TPU v7x, 32 devices: a whole 2x2x4 slice. The times are simulated.
32 devices in a mesh: ctx: 16 (over z, y, core), tp: 2 (over x).
Axes of the slice: x: 2, y: 2, z: 4, core: 2. Of those that a mesh axis runs over, the one named last changes fastest.
Arguments:
- queries: bfloat16 [1024, 1536], P('ctx', 'tp'), may hold values from -512 to 512
- keys: bfloat16 [1024, 1536], P('ctx', 'tp'), may hold values from -8 to 8
- values: bfloat16 [1024, 1536], P('ctx', 'tp'), may hold values from -6 to 6
- wo: bfloat16 [1536, 3072], P('tp'), may hold values from -0.15625 to 0.15625
- frame_tokens: int32 [16], replicated, may hold values from 32 to 64, as said below
Outputs:
- projected: bfloat16 [1024, 3072], P(('ctx', 'tp'))
Inputs may be any that keep to these rules, and one draw needn't show every extreme that they name: `frame_tokens`: at least 32 tokens of every frame are live.
All inputs are finite; a program needn't handle non-finite values.
Results may differ from a plain program's by a relative error of at most 0.014.
Values may be sent and summed in bfloat16 or wider, within the bound.
A program may use at most 128 MiB of HBM per device.

v0:
```python
import math

import jax
import jax.numpy as jnp
from jax import lax
from jax.sharding import PartitionSpec as P

HEAD_DIM = 128
FRAME = 64


def lookup_counts(frame_index, frame_tokens):
    frame_ids = jnp.arange(frame_tokens.shape[0], dtype=jnp.int32)
    picked = jnp.where(frame_index[:, None] == frame_ids[None, :], frame_tokens[None, :], 0)
    return jnp.sum(picked, axis=1)


def piece_update(
    state, query_rows, query_frames, key_piece, value_piece, frame_tokens, lower, upper
):
    run_max, run_total, run_acc = state
    count = key_piece.shape[0]
    head_count = query_rows.shape[1]
    key_pos = jnp.arange(count, dtype=jnp.int32)
    key_frame = key_pos // FRAME
    key_live = (
        (key_pos % FRAME < lookup_counts(key_frame, frame_tokens))
        & (key_pos >= lower)
        & (key_pos < upper)
    )
    key_heads = key_piece.reshape(count, head_count, HEAD_DIM)
    value_heads = value_piece.reshape(count, head_count, HEAD_DIM)
    scores = jnp.einsum("qhd,khd->hqk", query_rows, key_heads, preferred_element_type=jnp.float32)
    scores = scores * (1.0 / math.sqrt(HEAD_DIM))
    allowed = (key_frame[None, :] <= query_frames[:, None]) & key_live[None, :]
    scores = jnp.where(allowed[None], scores, -jnp.inf)
    new_max = jnp.maximum(run_max, jnp.max(scores, axis=-1))
    weights = jnp.exp(scores - new_max[:, :, None])
    new_total = jnp.sum(weights, axis=-1)
    added = jnp.einsum(
        "hqk,khd->qhd",
        weights.astype(jnp.bfloat16),
        value_heads,
        preferred_element_type=jnp.float32,
    )
    return (new_max, new_total, added)


def on_device(queries, keys, values, wo, frame_tokens):
    tok_rows = queries.shape[0]
    head_count = queries.shape[1] // HEAD_DIM
    ctx_size = lax.axis_size("ctx")
    ctx_index = lax.axis_index("ctx")
    all_rows = ctx_size * tok_rows
    row_offsets = jnp.arange(tok_rows, dtype=jnp.int32)
    query_pos = ctx_index * tok_rows + row_offsets
    query_frames = query_pos // FRAME
    query_rows = queries.reshape(tok_rows, head_count, HEAD_DIM)

    def empty_state():
        return (
            jnp.full((head_count, tok_rows), -1e30, jnp.float32),
            jnp.zeros((head_count, tok_rows), jnp.float32),
            jnp.zeros((tok_rows, head_count, HEAD_DIM), jnp.float32),
        )

    own_lower = jnp.int32(0)
    own_upper = jnp.int32(all_rows)
    own_state = empty_state()
    guest_state = empty_state()
    key_piece = lax.all_gather(keys, "ctx", axis=0, tiled=True)
    value_piece = lax.all_gather(values, "ctx", axis=0, tiled=True)
    own_state = piece_update(
        own_state,
        query_rows,
        query_frames,
        key_piece,
        value_piece,
        frame_tokens,
        own_lower,
        own_upper,
    )
    own_state, guest_state = (own_state, guest_state)
    run_max, run_total, run_acc = own_state
    heads_out = run_acc / jnp.transpose(run_total)[:, :, None]
    query_live = query_pos % FRAME < lookup_counts(query_frames, frame_tokens)
    heads_out = jnp.where(query_live[:, None, None], heads_out, 0.0)
    attended = heads_out.astype(jnp.bfloat16).reshape(tok_rows, head_count * HEAD_DIM)
    return lax.psum_scatter(
        jnp.dot(attended, wo, preferred_element_type=jnp.float32).astype(jnp.bfloat16),
        "tp",
        scatter_dimension=0,
        tiled=True,
    )


def solution(mesh):
    in_specs = (P("ctx", "tp"), P("ctx", "tp"), P("ctx", "tp"), P("tp", None), P())
    out_specs = P(("ctx", "tp"), None)
    return jax.shard_map(
        on_device, mesh=mesh, in_specs=in_specs, out_specs=out_specs, check_vma=False
    )
```

profile of v0, /device:TPU:16, one launch (start us, length us, event | category | flops | bytes accessed | tf_op | source)
XLA Modules:
  0.0 116.0 jit_solution(10007556777691750764)
XLA Ops:
  6.5 0.0 copy-start
  6.5 0.0 all-gather.3.cloned.1.call-start
  6.5 0.7 all-gather.3.cloned.1.call-update
  7.3 0.0 all-gather.5.cloned.1.call-start
  7.3 0.7 all-gather.5.cloned.1.call-update
  8.0 0.0 reduce-scatter.2.cloned.1.call-start
  8.1 0.7 select_reduce_fusion.1
  8.8 0.7 select_reduce_fusion
  9.6 0.1 compare_and_fusion
  9.7 38.8 %all-gather.3.cloned.1.call-done = bf16[1024,768]{1,0:T(8,128)(2,1)} async-done(((bf16[64,768]{1,0:T(8,128)(2,1)}), bf16[1024,768]{1,0:T(8,128)(2,1)}) %all-gather.3.cloned.1.call-update) | async-done | bytes 1572880 | tf_op jit(solution)/shard_map/all_gather | solution.py:71
  48.5 1.7 %copy.19 = bf16[1024,768]{0,1:T(8,128)(2,1)S(1)} copy(bf16[1024,768]{1,0:T(8,128)(2,1)} %all-gather.3.cloned.1.call-done) | data formatting | bytes 3145728 | tf_op jit(solution)/shard_map/all_gather | solution.py:71
  50.2 0.0 copy-done
  50.2 0.5 fusion.22
  50.7 0.4 fusion
  51.1 38.0 %all-gather.5.cloned.1.call-done = bf16[1024,768]{1,0:T(8,128)(2,1)} async-done(((bf16[64,768]{1,0:T(8,128)(2,1)}), bf16[1024,768]{1,0:T(8,128)(2,1)}) %all-gather.5.cloned.1.call-update) | async-done | bytes 1572880 | tf_op jit(solution)/shard_map/all_gather | solution.py:72
  89.1 1.7 %copy.22 = bf16[1024,768]{0,1:T(8,128)(2,1)S(1)} copy(bf16[1024,768]{1,0:T(8,128)(2,1)} %all-gather.5.cloned.1.call-done) | data formatting | bytes 3145728 | tf_op jit(solution)/shard_map/all_gather | solution.py:72
  90.8 0.7 fusion.5
  91.5 4.0 %convolution_convert_fusion = bf16[64,3072]{1,0:T(8,128)(2,1)} fusion(bf16[768,3072]{1,0:T(8,128)(2,1)} %param.8, bf16[6,8,8,128]{3,2,1,0:T(8,128)(2,1)S(1)} %fusion.5), kind=kOutput, calls=%fused_computation | convolution fusion | flops 302186496 | bytes 5210112 | tf_op jit(solution)/shard_map/dot_general | solution.py:90
  95.6 0.0 reduce-scatter.2.cloned.1.call-update
  95.6 13.9 %reduce-scatter.2.cloned.1.call-done = bf16[32,3072]{1,0:T(8,128)(2,1)} async-done(((bf16[64,3072]{1,0:T(8,128)(2,1)}), bf16[32,3072]{1,0:T(8,128)(2,1)}) %reduce-scatter.2.cloned.1.call-update) | async-done | bytes 196624 | tf_op jit(solution)/shard_map/reduce_scatter | solution.py:89
  (5 shorter events, 0.0 us)
Async XLA Ops:
  6.5 43.7 %copy-start = (bf16[64,768]{1,0:T(8,128)(2,1)S(1)}, bf16[64,768]{1,0:T(8,128)(2,1)}, u32[]{:S(2)}) copy-start(bf16[64,768]{1,0:T(8,128)(2,1)} %param.5) | copy-start | bytes 294916
  6.5 41.9 %all-gather.3.cloned.1.call-start = ((), (), s32[]{:S(2)}) async-start(), calls=%async_computation.1 | async-start | bytes 1671168 | tf_op jit(solution)/shard_map/all_gather | solution.py:71
  7.3 81.8 %all-gather.5.cloned.1.call-start = ((), (), s32[]{:S(2)}) async-start(), calls=%async_computation.2 | async-start | bytes 1671168 | tf_op jit(solution)/shard_map/all_gather | solution.py:72
  8.0 101.5 %reduce-scatter.2.cloned.1.call-start = ((), (), s32[]{:S(2)}) async-start(), calls=%async_computation.3 | async-start | bytes 589824 | tf_op jit(solution)/shard_map/reduce_scatter | solution.py:89
Sparse Core Ops, SparseCore 0:
  9.6 38.8 all-gather.2
  50.8 38.2 all-gather.4
  95.7 13.7 reduce-scatter.1
where the time goes:
time: 118 us; the launch traced here: 116 us
  waiting for transfers between devices  92.1 us (78%)
  between operations  13.2 us (11%)
  matrix products  5.26 us (4%)
  local copies, waits for them, and re-layouts  3.42 us (3%)
  other arithmetic  2 us (2%)
    all_gather x1, waiting for transfers between devices, on_device(): key_piece = lax.all_gather(keys, 'ctx', axis=0, tiled=True)  38.8 us
    all_gather x1, waiting for transfers between devices, on_device(): value_piece = lax.all_gather(values, 'ctx', axis=0, tiled=True)  38 us
    reduce_scatter x1, waiting for transfers between devices, on_device(): lax.psum_scatter(jnp.dot(attended, wo, preferred_element_type=jnp.float32...  13.9 us
    dot_general x1, matrix products, on_device(): jnp.dot(attended, wo, preferred_element_type=jnp.float32)  4.04 us
  transfers between devices with their start and end apart: 3, of which 3 were waited for; matrix products, arithmetic and copies ran while one was open for 4% of the time, Pallas kernels for 0%

commit v1 on v0

v1 whole, which is shorter than its diff:
```python
import functools
import math

import jax
import jax.numpy as jnp
from jax import lax
from jax.experimental import pallas as pl
from jax.experimental.pallas import tpu as pltpu
from jax.sharding import PartitionSpec as P

HEAD_DIM = 128
LAYER = 4
NEG = -1e30
MESH = pl.DeviceIdType.MESH
UP, SIDE, CORE, CROSS = 0, 1, 2, 3


def kernel(
    n,
    chunk,
    counts_ref,
    q_ref,
    k_hbm,
    v_hbm,
    wo_hbm,
    out_ref,
    k_all,
    v_all,
    wo_all,
    run_max,
    run_total,
    run_acc,
    attended,
    kept,
    outgoing,
    incoming,
    send_sem,
    recv_sem,
    local_sem,
    wo_sem,
    x_send_sem,
    x_recv_sem,
):
    tok_rows, columns = q_ref.shape
    head_count = columns // HEAD_DIM
    width = wo_hbm.shape[1]
    half = tok_rows // 2
    me = lax.axis_index("ctx")
    tp = lax.axis_index("tp")
    levels = n // LAYER
    level = me // LAYER
    lane = lax.rem(me, LAYER)
    base = level * LAYER
    side_y = lax.rem(lane + 2, LAYER)
    core_lane = lane + 1 - 2 * lax.rem(lane, 2)
    cross_lane = lax.rem(core_lane + 2, LAYER)
    above = lax.rem(me + LAYER, n)
    below = lax.rem(me + n - LAYER, n)
    has_above = level < levels - 1
    has_below = level > 0
    side_dev, core_dev = base + side_y, base + core_lane
    halls = (k_all, v_all)
    inputs = (k_hbm, v_hbm)

    wo_copy = pltpu.make_async_copy(wo_hbm, wo_all, wo_sem)
    wo_copy.start()

    def rows_of(src):
        return pl.ds(pl.multiple_of(src * tok_rows, tok_rows), tok_rows)

    own = [
        pltpu.make_async_copy(inputs[p], halls[p].at[rows_of(me)], local_sem.at[p])
        for p in range(2)
    ]
    for p in range(2):
        own[p].start()

    barrier = pltpu.get_barrier_semaphore()

    def greet(dev, other_tp):
        pl.semaphore_signal(barrier, inc=1, device_id=(dev, other_tp), device_id_type=MESH)

    @pl.when(has_above)
    def _():
        greet(above, tp)

    @pl.when(has_below)
    def _():
        greet(below, tp)

    greet(side_dev, tp)
    greet(core_dev, tp)
    greet(me, 1 - tp)
    pl.semaphore_wait(
        barrier, 3 + has_above.astype(jnp.int32) + has_below.astype(jnp.int32)
    )

    def piece(p, kind, step, src, dev):
        return pltpu.make_async_remote_copy(
            src_ref=halls[p].at[rows_of(src)],
            dst_ref=halls[p].at[rows_of(src)],
            send_sem=send_sem.at[kind, p, step],
            recv_sem=recv_sem.at[p, src],
            device_id=(dev, tp),
            device_id_type=MESH,
        )

    def forward_chain(step):
        src = me - LAYER * step
        for p in range(2):

            @pl.when(step > 0)
            def _():
                piece(p, UP, step, src, above).wait_recv()

            @pl.when(step == 0)
            def _():
                own[p].wait()

            @pl.when(has_above)
            def _():
                piece(p, UP, step, src, above).start()

            piece(p, SIDE, step, src, side_dev).start()
            piece(p, CORE, step, src, core_dev).start()

    def forward_side(step):
        src = base + side_y - LAYER * step
        for p in range(2):
            piece(p, CROSS, step, src, core_dev).wait_recv()
            piece(p, CROSS, step, src, core_dev).start()

    def wait_core(step):
        for p in range(2):
            for other in (core_lane, cross_lane):
                piece(p, CORE, step, base + other - LAYER * step, core_dev).wait_recv()

    span = LAYER * tok_rows
    col = lax.broadcasted_iota(jnp.int32, (tok_rows, span), 1)
    slot = col // tok_rows
    place = lax.rem(col, tok_rows)
    scale = 1.0 / math.sqrt(HEAD_DIM)

    def attend(step):
        first = base - LAYER * step
        limit = jnp.zeros((tok_rows, span), jnp.int32)
        for f in range(LAYER):
            live = jnp.where(first + f <= me, counts_ref[first + f], 0)
            limit = jnp.where(slot == f, live, limit)
        allowed = place < limit
        keys_at = pl.ds(pl.multiple_of(first * tok_rows, span), span)
        for h in range(head_count):
            cols = slice(h * HEAD_DIM, (h + 1) * HEAD_DIM)
            scores = lax.dot_general(
                q_ref[:, cols],
                k_all[keys_at, cols],
                (((1,), (1,)), ((), ())),
                preferred_element_type=jnp.float32,
            )
            scores = jnp.where(allowed, scores * scale, NEG)
            old_max = run_max[h][:, :1]
            new_max = jnp.maximum(old_max, jnp.max(scores, axis=-1, keepdims=True))
            fade = jnp.exp(old_max - new_max)
            weights = jnp.exp(scores - new_max)
            total = fade * run_total[h][:, :1] + jnp.sum(weights, axis=-1, keepdims=True)
            run_max[h] = jnp.broadcast_to(new_max, (tok_rows, HEAD_DIM))
            run_total[h] = jnp.broadcast_to(total, (tok_rows, HEAD_DIM))
            run_acc[:, cols] = fade * run_acc[:, cols] + jnp.dot(
                weights.astype(jnp.bfloat16),
                v_all[keys_at, cols],
                preferred_element_type=jnp.float32,
            )

    run_max[...] = jnp.full(run_max.shape, NEG, jnp.float32)
    run_total[...] = jnp.zeros(run_total.shape, jnp.float32)
    run_acc[...] = jnp.zeros(run_acc.shape, jnp.float32)

    forward_chain(0)
    forward_side(0)

    def body(step, carry):
        forward_chain(step)
        wait_core(step - 1)
        attend(step - 1)
        forward_side(step)
        return carry

    lax.fori_loop(1, level + 1, body, 0)
    wait_core(level)
    attend(level)

    row = lax.broadcasted_iota(jnp.int32, (tok_rows, HEAD_DIM), 0)
    row_live = row < counts_ref[me]
    for h in range(head_count):
        cols = slice(h * HEAD_DIM, (h + 1) * HEAD_DIM)
        out = jnp.where(row_live, run_acc[:, cols] / run_total[h], 0.0)
        attended[:, cols] = out.astype(jnp.bfloat16)

    wo_copy.wait()
    theirs = attended[pl.ds(pl.multiple_of((1 - tp) * half, half), half), :]
    mine = attended[pl.ds(pl.multiple_of(tp * half, half), half), :]
    lhs = jnp.concatenate([theirs, mine], axis=0)

    def swap(c):
        return pltpu.make_async_remote_copy(
            src_ref=outgoing.at[c],
            dst_ref=incoming.at[c],
            send_sem=x_send_sem.at[c],
            recv_sem=x_recv_sem.at[c],
            device_id=(me, 1 - tp),
            device_id_type=MESH,
        )

    for c in range(width // chunk):
        part = jnp.dot(
            lhs, wo_all[:, c * chunk : (c + 1) * chunk], preferred_element_type=jnp.float32
        )
        outgoing[c] = part[:half].astype(jnp.bfloat16)
        swap(c).start()
        kept[c] = part[half:]

    def drain(step, carry):
        for p in range(2):

            @pl.when(has_above)
            def _():
                piece(p, UP, step, me - LAYER * step, above).wait_send()

            piece(p, SIDE, step, me - LAYER * step, side_dev).wait_send()
            piece(p, CORE, step, me - LAYER * step, core_dev).wait_send()
            piece(p, CROSS, step, me - LAYER * step, core_dev).wait_send()
        return carry

    lax.fori_loop(0, level + 1, drain, 0)
    for c in range(width // chunk):
        swap(c).wait_recv()
        out_ref[:, c * chunk : (c + 1) * chunk] = (
            kept[c] + incoming[c].astype(jnp.float32)
        ).astype(out_ref.dtype)
    for c in range(width // chunk):
        swap(c).wait_send()


def on_device(queries, keys, values, wo, frame_tokens):
    tok_rows, columns = queries.shape
    width = wo.shape[1]
    n = lax.axis_size("ctx")
    half = tok_rows // 2
    chunk = 512 if width % 512 == 0 else width
    chunks = width // chunk
    head_count = columns // HEAD_DIM
    levels = n // LAYER
    vmem = pltpu.VMEM
    dma = pltpu.SemaphoreType.DMA
    return pl.pallas_call(
        functools.partial(kernel, n, chunk),
        out_shape=jax.ShapeDtypeStruct((half, width), jnp.bfloat16),
        in_specs=[
            pl.BlockSpec(memory_space=pltpu.SMEM),
            pl.BlockSpec(memory_space=vmem),
            pl.BlockSpec(memory_space=pl.ANY),
            pl.BlockSpec(memory_space=pl.ANY),
            pl.BlockSpec(memory_space=pl.ANY),
        ],
        out_specs=pl.BlockSpec(memory_space=vmem),
        scratch_shapes=[
            vmem((n * tok_rows, columns), jnp.bfloat16),
            vmem((n * tok_rows, columns), jnp.bfloat16),
            vmem(wo.shape, jnp.bfloat16),
            vmem((head_count, tok_rows, HEAD_DIM), jnp.float32),
            vmem((head_count, tok_rows, HEAD_DIM), jnp.float32),
            vmem((tok_rows, columns), jnp.float32),
            vmem((tok_rows, columns), jnp.bfloat16),
            vmem((chunks, half, chunk), jnp.float32),
            vmem((chunks, half, chunk), jnp.bfloat16),
            vmem((chunks, half, chunk), jnp.bfloat16),
            dma((4, 2, levels)),
            dma((2, n)),
            dma((2,)),
            dma,
            dma((chunks,)),
            dma((chunks,)),
        ],
        compiler_params=pltpu.CompilerParams(
            collective_id=0, has_side_effects=True, vmem_limit_bytes=52 << 20
        ),
    )(frame_tokens, queries, keys, values, wo)


def solution(mesh):
    in_specs = (P("ctx", "tp"), P("ctx", "tp"), P("ctx", "tp"), P("tp", None), P())
    out_specs = P(("ctx", "tp"), None)
    return jax.shard_map(
        on_device, mesh=mesh, in_specs=in_specs, out_specs=out_specs, check_vma=False
    )
```

time: 118 us -> 37.5 us (0.32)
  the two profiles are of different devices: /device:TPU:16 before, /device:TPU:25 now
where the time goes in v1:
time: 37.5 us; the launch traced here: 37.3 us
  Pallas kernels  33.3 us (89%)
  local copies, waits for them, and re-layouts  4.01 us (11%)
    pallas_call x1, Pallas kernels, on_device(): pl.pallas_call(functools.partial(kernel, n, chunk), out_shape=jax.ShapeDt...  33.3 us
    unnamed x9, local copies, waits for them, and re-layouts  4.01 us

profile of v1, /device:TPU:25, one launch (start us, length us, event | category | flops | bytes accessed | tf_op | source)
XLA Modules:
  0.0 37.3 jit_solution(10204563819682982533)
XLA Ops:
  0.0 0.0 copy-start
  0.0 0.9 %copy-done = bf16[64,768]{1,0:T(8,128)(2,1)S(1)} copy-done((bf16[64,768]{1,0:T(8,128)(2,1)S(1)}, bf16[64,768]{1,0:T(8,128)(2,1)}, u32[]{:S(2)}) %copy-start) | copy-done | bytes 98328
  0.9 0.0 copy-start.1
  0.9 0.9 %copy-done.1 = bf16[64,768]{1,0:T(8,128)(2,1)S(1)} copy-done((bf16[64,768]{1,0:T(8,128)(2,1)S(1)}, bf16[64,768]{1,0:T(8,128)(2,1)}, u32[]{:S(2)}) %copy-start.1) | copy-done | bytes 98328
  1.8 0.0 copy-start.2
  1.8 0.9 %copy-done.2 = bf16[64,768]{1,0:T(8,128)(2,1)S(1)} copy-done((bf16[64,768]{1,0:T(8,128)(2,1)S(1)}, bf16[64,768]{1,0:T(8,128)(2,1)}, u32[]{:S(2)}) %copy-start.2) | copy-done | bytes 98328
  2.7 0.0 copy-start.3
  2.7 0.7 %copy-done.3 = s32[16]{0:T(128)S(1)} copy-done((s32[16]{0:T(128)S(1)}, s32[16]{0:T(128)}, u32[]{:S(2)}) %copy-start.3) | copy-done | bytes 88
  3.3 33.3 %shard_map.55 = bf16[32,3072]{1,0:T(8,128)(2,1)S(1)} custom-call(s32[16]{0:T(128)S(1)} %copy-done.3, bf16[64,768]{1,0:T(8,128)(2,1)S(1)} %copy-done, bf16[64,768]{1,0:T(8,128)(2,1)S(1)} %copy-done.1, bf16[64,768]{1,0:T(8,128)(2,1)S(1)} %copy-done.2, bf16[768,3072]{1,0:T(8,128)(2,1)} %wo_hbm.1), custom_call_target="tpu_custom_call" | custom-call | tf_op jit(solution)/shard_map/pallas_call | solution.py:255
  36.6 0.7 %copy.7 = bf16[32,3072]{1,0:T(8,128)(2,1)} copy(bf16[32,3072]{1,0:T(8,128)(2,1)S(1)} %shard_map.55) | data formatting | bytes 393216
Async XLA Ops:
  0.0 0.9 %copy-start = (bf16[64,768]{1,0:T(8,128)(2,1)S(1)}, bf16[64,768]{1,0:T(8,128)(2,1)}, u32[]{:S(2)}) copy-start(bf16[64,768]{1,0:T(8,128)(2,1)} %q_ref.1) | copy-start | bytes 294916
  0.9 0.9 %copy-start.1 = (bf16[64,768]{1,0:T(8,128)(2,1)S(1)}, bf16[64,768]{1,0:T(8,128)(2,1)}, u32[]{:S(2)}) copy-start(bf16[64,768]{1,0:T(8,128)(2,1)} %k_hbm.1) | copy-start | bytes 294916
  1.8 0.9 %copy-start.2 = (bf16[64,768]{1,0:T(8,128)(2,1)S(1)}, bf16[64,768]{1,0:T(8,128)(2,1)}, u32[]{:S(2)}) copy-start(bf16[64,768]{1,0:T(8,128)(2,1)} %v_hbm.1) | copy-start | bytes 294916
  2.7 0.7 %copy-start.3 = (s32[16]{0:T(128)S(1)}, s32[16]{0:T(128)}, u32[]{:S(2)}) copy-start(s32[16]{0:T(128)} %counts_ref.1) | copy-start | bytes 196

commit v2 on v1

--- a/solution.py
+++ b/solution.py
@@ -13,6 +13,10 @@
 NEG = -1e30
 MESH = pl.DeviceIdType.MESH
 UP, SIDE, CORE, CROSS = 0, 1, 2, 3
+
+
+def group_levels(levels):
+    return levels // 2 if levels % 2 == 0 else levels
 
 
 def kernel(
@@ -30,6 +34,11 @@
     run_max,
     run_total,
     run_acc,
+    guest_q,
+    guest_acc,
+    guest_stats,
+    far_acc,
+    far_stats,
     attended,
     kept,
     outgoing,
@@ -40,6 +49,10 @@
     wo_sem,
     x_send_sem,
     x_recv_sem,
+    q_send_sem,
+    q_recv_sem,
+    back_send_sem,
+    back_recv_sem,
 ):
     tok_rows, columns = q_ref.shape
     head_count = columns // HEAD_DIM
@@ -48,7 +61,12 @@
     me = lax.axis_index("ctx")
     tp = lax.axis_index("tp")
     levels = n // LAYER
+    group = group_levels(levels)
+    guests = levels - group
     level = me // LAYER
+    is_upper = level >= group
+    local = lax.rem(level, group)
+    is_host = level == (group - 1 if guests else levels)
     lane = lax.rem(me, LAYER)
     base = level * LAYER
     side_y = lax.rem(lane + 2, LAYER)
@@ -56,8 +74,10 @@
     cross_lane = lax.rem(core_lane + 2, LAYER)
     above = lax.rem(me + LAYER, n)
     below = lax.rem(me + n - LAYER, n)
-    has_above = level < levels - 1
-    has_below = level > 0
+    has_above = local < group - 1
+    has_below = local > 0
+    host = (group - 1) * LAYER + lane
+    guest_slot = lax.rem(level, group)
     side_dev, core_dev = base + side_y, base + core_lane
     halls = (k_all, v_all)
     inputs = (k_hbm, v_hbm)
@@ -91,9 +111,54 @@
     greet(side_dev, tp)
     greet(core_dev, tp)
     greet(me, 1 - tp)
+
+    @pl.when(is_upper)
+    def _():
+        greet(host, tp)
+
+    @pl.when(is_host)
+    def _():
+        def greet_guest(j, carry):
+            greet(me + LAYER * (1 + j), tp)
+            return carry
+
+        lax.fori_loop(0, guests, greet_guest, 0)
+
     pl.semaphore_wait(
-        barrier, 3 + has_above.astype(jnp.int32) + has_below.astype(jnp.int32)
+        barrier,
+        3
+        + has_above.astype(jnp.int32)
+        + has_below.astype(jnp.int32)
+        + is_upper.astype(jnp.int32)
+        + guests * is_host.astype(jnp.int32),
     )
+
+    def ask(j):
+        return pltpu.make_async_remote_copy(
+            src_ref=q_ref,
+            dst_ref=guest_q.at[j],
+            send_sem=q_send_sem,
+            recv_sem=q_recv_sem.at[j],
+            device_id=(host, tp),
+            device_id_type=MESH,
+        )
+
+    def answer(j, p):
+        source, target = ((guest_acc.at[j], far_acc), (guest_stats.at[j], far_stats))[p]
+        return pltpu.make_async_remote_copy(
+            src_ref=source,
+            dst_ref=target,
+            send_sem=back_send_sem.at[p, j],
+            recv_sem=back_recv_sem.at[p],
+            device_id=(lax.rem(me + LAYER * (1 + j), n), tp),
+            device_id_type=MESH,
+        )
+
+    if guests:
+
+        @pl.when(is_upper)
+        def _():
+            ask(guest_slot).start()
 
     def piece(p, kind, step, src, dev):
         return pltpu.make_async_remote_copy(
@@ -141,36 +206,70 @@
     place = lax.rem(col, tok_rows)
     scale = 1.0 / math.sqrt(HEAD_DIM)
 
-    def attend(step):
+    def attend(step, state, load_query, causal):
         first = base - LAYER * step
         limit = jnp.zeros((tok_rows, span), jnp.int32)
         for f in range(LAYER):
-            live = jnp.where(first + f <= me, counts_ref[first + f], 0)
+            live = counts_ref[first + f]
+            if causal:
+                live = jnp.where(first + f <= me, live, 0)
             limit = jnp.where(slot == f, live, limit)
         allowed = place < limit
         keys_at = pl.ds(pl.multiple_of(first * tok_rows, span), span)
         for h in range(head_count):
             cols = slice(h * HEAD_DIM, (h + 1) * HEAD_DIM)
             scores = lax.dot_general(
-                q_ref[:, cols],
+                load_query(cols),
                 k_all[keys_at, cols],
                 (((1,), (1,)), ((), ())),
                 preferred_element_type=jnp.float32,
             )
             scores = jnp.where(allowed, scores * scale, NEG)
-            old_max = run_max[h][:, :1]
+            old_max = run_max[state, h][:, :1]
             new_max = jnp.maximum(old_max, jnp.max(scores, axis=-1, keepdims=True))
             fade = jnp.exp(old_max - new_max)
             weights = jnp.exp(scores - new_max)
-            total = fade * run_total[h][:, :1] + jnp.sum(weights, axis=-1, keepdims=True)
-            run_max[h] = jnp.broadcast_to(new_max, (tok_rows, HEAD_DIM))
-            run_total[h] = jnp.broadcast_to(total, (tok_rows, HEAD_DIM))
-            run_acc[:, cols] = fade * run_acc[:, cols] + jnp.dot(
+            total = fade * run_total[state, h][:, :1] + jnp.sum(weights, axis=-1, keepdims=True)
+            run_max[state, h] = jnp.broadcast_to(new_max, (tok_rows, HEAD_DIM))
+            run_total[state, h] = jnp.broadcast_to(total, (tok_rows, HEAD_DIM))
+            run_acc[state, :, cols] = fade * run_acc[state, :, cols] + jnp.dot(
                 weights.astype(jnp.bfloat16),
                 v_all[keys_at, cols],
                 preferred_element_type=jnp.float32,
             )
 
+    def attend_own(step):
+        attend(step, 0, lambda cols: q_ref[:, cols], True)
+
+    spot = lax.broadcasted_iota(jnp.int32, (tok_rows, HEAD_DIM), 1)
+
+    def attend_guests(step, last):
+        if not guests:
+            return
+
+        @pl.when(is_host)
+        def _():
+            def one(i, carry):
+                j = guests - 1 - i
+
+                @pl.when(step == 0)
+                def _():
+                    ask(j).wait_recv()
+
+                attend(step, 1 + j, lambda cols: guest_q[j, :, cols], False)
+                if last:
+                    stats = jnp.zeros((tok_rows, HEAD_DIM), jnp.float32)
+                    for h in range(head_count):
+                        stats = jnp.where(spot == h, run_max[1 + j, h], stats)
+                        stats = jnp.where(spot == head_count + h, run_total[1 + j, h], stats)
+                    guest_stats[j] = stats
+                    guest_acc[j] = run_acc[1 + j].astype(jnp.bfloat16)
+                    answer(j, 1).start()
+                    answer(j, 0).start()
+                return carry
+
+            lax.fori_loop(0, guests, one, 0)
+
     run_max[...] = jnp.full(run_max.shape, NEG, jnp.float32)
     run_total[...] = jnp.zeros(run_total.shape, jnp.float32)
     run_acc[...] = jnp.zeros(run_acc.shape, jnp.float32)
@@ -181,19 +280,40 @@
     def body(step, carry):
         forward_chain(step)
         wait_core(step - 1)
-        attend(step - 1)
+        attend_own(step - 1)
         forward_side(step)
+        attend_guests(step - 1, False)
         return carry
 
-    lax.fori_loop(1, level + 1, body, 0)
-    wait_core(level)
-    attend(level)
+    lax.fori_loop(1, local + 1, body, 0)
+    wait_core(local)
+    attend_guests(local, True)
+    attend_own(local)
+
+    if guests:
+
+        @pl.when(is_upper)
+        def _():
+            answer(0, 1).wait_recv()
+            answer(0, 0).wait_recv()
+            for h in range(head_count):
+                cols = slice(h * HEAD_DIM, (h + 1) * HEAD_DIM)
+                far_max = far_stats[:, h : h + 1]
+                far_total = far_stats[:, head_count + h : head_count + h + 1]
+                old_max = run_max[0, h][:, :1]
+                new_max = jnp.maximum(old_max, far_max)
+                fade, far_fade = jnp.exp(old_max - new_max), jnp.exp(far_max - new_max)
+                total = fade * run_total[0, h][:, :1] + far_fade * far_total
+                run_total[0, h] = jnp.broadcast_to(total, (tok_rows, HEAD_DIM))
+                run_acc[0, :, cols] = fade * run_acc[0, :, cols] + far_fade * far_acc[
+                    :, cols
+                ].astype(jnp.float32)
 
     row = lax.broadcasted_iota(jnp.int32, (tok_rows, HEAD_DIM), 0)
     row_live = row < counts_ref[me]
     for h in range(head_count):
         cols = slice(h * HEAD_DIM, (h + 1) * HEAD_DIM)
-        out = jnp.where(row_live, run_acc[:, cols] / run_total[h], 0.0)
+        out = jnp.where(row_live, run_acc[0, :, cols] / run_total[0, h], 0.0)
         attended[:, cols] = out.astype(jnp.bfloat16)
 
     wo_copy.wait()
@@ -231,7 +351,22 @@
             piece(p, CROSS, step, me - LAYER * step, core_dev).wait_send()
         return carry
 
-    lax.fori_loop(0, level + 1, drain, 0)
+    lax.fori_loop(0, local + 1, drain, 0)
+    if guests:
+
+        @pl.when(is_upper)
+        def _():
+            ask(guest_slot).wait_send()
+
+        @pl.when(is_host)
+        def _():
+            def drain_guest(j, carry):
+                answer(j, 0).wait_send()
+                answer(j, 1).wait_send()
+                return carry
+
+            lax.fori_loop(0, guests, drain_guest, 0)
+
     for c in range(width // chunk):
         swap(c).wait_recv()
         out_ref[:, c * chunk : (c + 1) * chunk] = (
@@ -250,6 +385,8 @@
     chunks = width // chunk
     head_count = columns // HEAD_DIM
     levels = n // LAYER
+    guests = levels - group_levels(levels)
+    room = max(guests, 1)
     vmem = pltpu.VMEM
     dma = pltpu.SemaphoreType.DMA
     return pl.pallas_call(
@@ -258,18 +395,23 @@
         in_specs=[
             pl.BlockSpec(memory_space=pltpu.SMEM),
             pl.BlockSpec(memory_space=vmem),
-            pl.BlockSpec(memory_space=pl.ANY),
-            pl.BlockSpec(memory_space=pl.ANY),
-            pl.BlockSpec(memory_space=pl.ANY),
+            pl.BlockSpec(memory_space=pltpu.HBM),
+            pl.BlockSpec(memory_space=pltpu.HBM),
+            pl.BlockSpec(memory_space=pltpu.HBM),
         ],
         out_specs=pl.BlockSpec(memory_space=vmem),
         scratch_shapes=[
             vmem((n * tok_rows, columns), jnp.bfloat16),
             vmem((n * tok_rows, columns), jnp.bfloat16),
             vmem(wo.shape, jnp.bfloat16),
-            vmem((head_count, tok_rows, HEAD_DIM), jnp.float32),
-            vmem((head_count, tok_rows, HEAD_DIM), jnp.float32),
-            vmem((tok_rows, columns), jnp.float32),
+            vmem((1 + guests, head_count, tok_rows, HEAD_DIM), jnp.float32),
+            vmem((1 + guests, head_count, tok_rows, HEAD_DIM), jnp.float32),
+            vmem((1 + guests, tok_rows, columns), jnp.float32),
+            vmem((room, tok_rows, columns), jnp.bfloat16),
+            vmem((room, tok_rows, columns), jnp.bfloat16),
+            vmem((room, tok_rows, HEAD_DIM), jnp.float32),
+            vmem((tok_rows, columns), jnp.bfloat16),
+            vmem((tok_rows, HEAD_DIM), jnp.float32),
             vmem((tok_rows, columns), jnp.bfloat16),
             vmem((chunks, half, chunk), jnp.float32),
             vmem((chunks, half, chunk), jnp.bfloat16),
@@ -280,9 +422,13 @@
             dma,
             dma((chunks,)),
             dma((chunks,)),
+            dma,
+            dma((room,)),
+            dma((2, room)),
+            dma((2,)),
         ],
         compiler_params=pltpu.CompilerParams(
-            collective_id=0, has_side_effects=True, vmem_limit_bytes=52 << 20
+            collective_id=0, has_side_effects=True, vmem_limit_bytes=67043328
         ),
     )(frame_tokens, queries, keys, values, wo)
 

time: 37.5 us -> 36.7 us (0.979)
  the two profiles are of different devices: /device:TPU:25 before, /device:TPU:16 now
where the time goes in v2:
time: 36.7 us; the launch traced here: 36.5 us
  Pallas kernels  34.9 us (95%)
  local copies, waits for them, and re-layouts  1.62 us (4%)
    pallas_call x1, Pallas kernels, on_device(): pl.pallas_call(functools.partial(kernel, n, chunk), out_shape=jax.ShapeDt...  34.9 us
    unnamed x1, local copies, waits for them, and re-layouts  1.62 us

profile of v2, /device:TPU:16, one launch (start us, length us, event | category | flops | bytes accessed | tf_op | source)
XLA Modules:
  0.0 36.5 jit_solution(12293918858181693402)
XLA Ops:
  0.0 34.9 %shard_map.55 = bf16[32,3072]{1,0:T(8,128)(2,1)} custom-call(s32[16]{0:T(128)} %counts_ref.1, bf16[64,768]{1,0:T(8,128)(2,1)} %q_ref.1, bf16[64,768]{1,0:T(8,128)(2,1)} %k_hbm.1, bf16[64,768]{1,0:T(8,128)(2,1)} %v_hbm.1, bf16[768,3072]{1,0:T(8,128)(2,1)} %wo_hbm.1), custom_call_target="tpu_custom_call" | custom-call | tf_op jit(solution)/shard_map/pallas_call | solution.py:392
  34.9 1.6 %copy.7 = bf16[32,3072]{1,0:T(8,128)(2,1)} copy(bf16[32,3072]{1,0:T(8,128)(2,1)} %shard_map.55) | data formatting | bytes 393216

commit v3 on v2

--- a/solution.py
+++ b/solution.py
@@ -32,9 +32,10 @@
     v_all,
     wo_all,
     run_max,
-    run_total,
     run_acc,
     guest_q,
+    guest_max,
+    guest_sum,
     guest_acc,
     guest_stats,
     far_acc,
@@ -136,7 +137,7 @@
     def ask(j):
         return pltpu.make_async_remote_copy(
             src_ref=q_ref,
-            dst_ref=guest_q.at[j],
+            dst_ref=guest_q.at[rows_of(j)],
             send_sem=q_send_sem,
             recv_sem=q_recv_sem.at[j],
             device_id=(host, tp),
@@ -201,14 +202,16 @@
                 piece(p, CORE, step, base + other - LAYER * step, core_dev).wait_recv()
 
     span = LAYER * tok_rows
-    col = lax.broadcasted_iota(jnp.int32, (tok_rows, span), 1)
+    col = lax.broadcasted_iota(jnp.int32, (1, span), 1)
     slot = col // tok_rows
     place = lax.rem(col, tok_rows)
-    scale = 1.0 / math.sqrt(HEAD_DIM)
-
-    def attend(step, state, load_query, causal):
+    scale = math.log2(math.e) / math.sqrt(HEAD_DIM)
+    ones = jnp.ones((span, HEAD_DIM), jnp.bfloat16)
+    head_cols = [slice(h * HEAD_DIM, (h + 1) * HEAD_DIM) for h in range(head_count)]
+
+    def attend(step, query, max_ref, acc_ref, rows, causal):
         first = base - LAYER * step
-        limit = jnp.zeros((tok_rows, span), jnp.int32)
+        limit = jnp.zeros((1, span), jnp.int32)
         for f in range(LAYER):
             live = counts_ref[first + f]
             if causal:
@@ -216,32 +219,43 @@
             limit = jnp.where(slot == f, live, limit)
         allowed = place < limit
         keys_at = pl.ds(pl.multiple_of(first * tok_rows, span), span)
-        for h in range(head_count):
-            cols = slice(h * HEAD_DIM, (h + 1) * HEAD_DIM)
-            scores = lax.dot_general(
-                load_query(cols),
+        scores = [
+            lax.dot_general(
+                query(cols),
                 k_all[keys_at, cols],
                 (((1,), (1,)), ((), ())),
                 preferred_element_type=jnp.float32,
             )
-            scores = jnp.where(allowed, scores * scale, NEG)
-            old_max = run_max[state, h][:, :1]
-            new_max = jnp.maximum(old_max, jnp.max(scores, axis=-1, keepdims=True))
-            fade = jnp.exp(old_max - new_max)
-            weights = jnp.exp(scores - new_max)
-            total = fade * run_total[state, h][:, :1] + jnp.sum(weights, axis=-1, keepdims=True)
-            run_max[state, h] = jnp.broadcast_to(new_max, (tok_rows, HEAD_DIM))
-            run_total[state, h] = jnp.broadcast_to(total, (tok_rows, HEAD_DIM))
-            run_acc[state, :, cols] = fade * run_acc[state, :, cols] + jnp.dot(
-                weights.astype(jnp.bfloat16),
-                v_all[keys_at, cols],
+            for cols in head_cols
+        ]
+        scores = [jnp.where(allowed, one, NEG) for one in scores]
+        old_max = [max_ref[h, rows, :][:, :1] for h in range(head_count)]
+        new_max = [
+            jnp.maximum(old, jnp.max(one, axis=-1, keepdims=True))
+            for old, one in zip(old_max, scores)
+        ]
+        weights = [
+            jnp.exp2((one - top) * scale).astype(jnp.bfloat16)
+            for one, top in zip(scores, new_max)
+        ]
+        added = [
+            jnp.dot(
+                one,
+                jnp.concatenate([v_all[keys_at, cols], ones], axis=1),
                 preferred_element_type=jnp.float32,
             )
+            for one, cols in zip(weights, head_cols)
+        ]
+        for h in range(head_count):
+            fade = jnp.exp2((old_max[h] - new_max[h]) * scale)
+            max_ref[h, rows, :] = jnp.broadcast_to(new_max[h], (fade.shape[0], HEAD_DIM))
+            acc_ref[h, rows, :] = fade * acc_ref[h, rows, :] + added[h]
 
     def attend_own(step):
-        attend(step, 0, lambda cols: q_ref[:, cols], True)
+        attend(step, lambda cols: q_ref[:, cols], run_max, run_acc, slice(0, tok_rows), True)
 
     spot = lax.broadcasted_iota(jnp.int32, (tok_rows, HEAD_DIM), 1)
+    pack = 2 if guests % 2 == 0 else 1
 
     def attend_guests(step, last):
         if not guests:
@@ -250,29 +264,44 @@
         @pl.when(is_host)
         def _():
             def one(i, carry):
-                j = guests - 1 - i
+                block = guests // pack - 1 - i
 
                 @pl.when(step == 0)
                 def _():
-                    ask(j).wait_recv()
-
-                attend(step, 1 + j, lambda cols: guest_q[j, :, cols], False)
+                    for g in range(pack):
+                        ask(block * pack + g).wait_recv()
+
+                rows = pl.ds(pl.multiple_of(block * pack * tok_rows, tok_rows), pack * tok_rows)
+                attend(
+                    step, lambda cols: guest_q[rows, cols], guest_max, guest_sum, rows, False
+                )
                 if last:
-                    stats = jnp.zeros((tok_rows, HEAD_DIM), jnp.float32)
-                    for h in range(head_count):
-                        stats = jnp.where(spot == h, run_max[1 + j, h], stats)
-                        stats = jnp.where(spot == head_count + h, run_total[1 + j, h], stats)
-                    guest_stats[j] = stats
-                    guest_acc[j] = run_acc[1 + j].astype(jnp.bfloat16)
-                    answer(j, 1).start()
-                    answer(j, 0).start()
+                    for g in reversed(range(pack)):
+                        j = block * pack + g
+                        at = rows_of(j)
+                        stats = jnp.zeros((tok_rows, HEAD_DIM), jnp.float32)
+                        for h in range(head_count):
+                            stats = jnp.where(spot == h, guest_max[h, at, :], stats)
+                            stats = jnp.where(
+                                spot == head_count + h, guest_sum[h, at, HEAD_DIM:], stats
+                            )
+                            guest_acc[j, :, head_cols[h]] = guest_sum[h, at, :HEAD_DIM].astype(
+                                jnp.bfloat16
+                            )
+                        guest_stats[j] = stats
+                        answer(j, 0).start()
+                        answer(j, 1).start()
                 return carry
 
-            lax.fori_loop(0, guests, one, 0)
+            lax.fori_loop(0, guests // pack, one, 0)
 
     run_max[...] = jnp.full(run_max.shape, NEG, jnp.float32)
-    run_total[...] = jnp.zeros(run_total.shape, jnp.float32)
     run_acc[...] = jnp.zeros(run_acc.shape, jnp.float32)
+
+    @pl.when(is_host)
+    def _():
+        guest_max[...] = jnp.full(guest_max.shape, NEG, jnp.float32)
+        guest_sum[...] = jnp.zeros(guest_sum.shape, jnp.float32)
 
     forward_chain(0)
     forward_side(0)
@@ -297,24 +326,26 @@
             answer(0, 1).wait_recv()
             answer(0, 0).wait_recv()
             for h in range(head_count):
-                cols = slice(h * HEAD_DIM, (h + 1) * HEAD_DIM)
                 far_max = far_stats[:, h : h + 1]
                 far_total = far_stats[:, head_count + h : head_count + h + 1]
-                old_max = run_max[0, h][:, :1]
+                old_max = run_max[h][:, :1]
                 new_max = jnp.maximum(old_max, far_max)
-                fade, far_fade = jnp.exp(old_max - new_max), jnp.exp(far_max - new_max)
-                total = fade * run_total[0, h][:, :1] + far_fade * far_total
-                run_total[0, h] = jnp.broadcast_to(total, (tok_rows, HEAD_DIM))
-                run_acc[0, :, cols] = fade * run_acc[0, :, cols] + far_fade * far_acc[
-                    :, cols
-                ].astype(jnp.float32)
+                fade = jnp.exp2((old_max - new_max) * scale)
+                far_fade = jnp.exp2((far_max - new_max) * scale)
+                far = jnp.concatenate(
+                    [
+                        far_acc[:, head_cols[h]].astype(jnp.float32),
+                        jnp.broadcast_to(far_total, (tok_rows, HEAD_DIM)),
+                    ],
+                    axis=1,
+                )
+                run_acc[h] = fade * run_acc[h] + far_fade * far
 
     row = lax.broadcasted_iota(jnp.int32, (tok_rows, HEAD_DIM), 0)
     row_live = row < counts_ref[me]
     for h in range(head_count):
-        cols = slice(h * HEAD_DIM, (h + 1) * HEAD_DIM)
-        out = jnp.where(row_live, run_acc[0, :, cols] / run_total[0, h], 0.0)
-        attended[:, cols] = out.astype(jnp.bfloat16)
+        out = jnp.where(row_live, run_acc[h, :, :HEAD_DIM] / run_acc[h, :, HEAD_DIM:], 0.0)
+        attended[:, head_cols[h]] = out.astype(jnp.bfloat16)
 
     wo_copy.wait()
     theirs = attended[pl.ds(pl.multiple_of((1 - tp) * half, half), half), :]
@@ -404,10 +435,11 @@
             vmem((n * tok_rows, columns), jnp.bfloat16),
             vmem((n * tok_rows, columns), jnp.bfloat16),
             vmem(wo.shape, jnp.bfloat16),
-            vmem((1 + guests, head_count, tok_rows, HEAD_DIM), jnp.float32),
-            vmem((1 + guests, head_count, tok_rows, HEAD_DIM), jnp.float32),
-            vmem((1 + guests, tok_rows, columns), jnp.float32),
-            vmem((room, tok_rows, columns), jnp.bfloat16),
+            vmem((head_count, tok_rows, HEAD_DIM), jnp.float32),
+            vmem((head_count, tok_rows, 2 * HEAD_DIM), jnp.float32),
+            vmem((room * tok_rows, columns), jnp.bfloat16),
+            vmem((head_count, room * tok_rows, HEAD_DIM), jnp.float32),
+            vmem((head_count, room * tok_rows, 2 * HEAD_DIM), jnp.float32),
             vmem((room, tok_rows, columns), jnp.bfloat16),
             vmem((room, tok_rows, HEAD_DIM), jnp.float32),
             vmem((tok_rows, columns), jnp.bfloat16),
@@ -428,9 +460,9 @@
             dma((2,)),
         ],
         compiler_params=pltpu.CompilerParams(
-            collective_id=0, has_side_effects=True, vmem_limit_bytes=67043328
+            collective_id=0, has_side_effects=True, vmem_limit_bytes=52 << 20
         ),
-    )(frame_tokens, queries, keys, values, wo)
+    )(*[pltpu.with_memory_space_constraint(x, pltpu.HBM) for x in (frame_tokens, queries, keys, values, wo)])
 
 
 def solution(mesh):

time: 36.7 us -> 32.4 us (0.88)
  Pallas kernels: 34.9 us -> 31.5 us
  local copies, waits for them, and re-layouts: 1.62 us -> 0.68 us
    pallas_call x1, Pallas kernels: 34.9 us -> 31.5 us  [on_device(): pl.pallas_call(functools.partial(kernel, n, chunk), out_shape=jax.ShapeDt...]
    unnamed x1, local copies, waits for them, and re-layouts: 1.62 us -> 0.68 us
where the time goes in v3:
time: 32.4 us; the launch traced here: 32.2 us
  Pallas kernels  31.5 us (97%)
  local copies, waits for them, and re-layouts  0.68 us (2%)
    pallas_call x1, Pallas kernels, on_device(): pl.pallas_call(functools.partial(kernel, n, chunk), out_shape=jax.ShapeDt...  31.5 us
    unnamed x1, local copies, waits for them, and re-layouts  0.68 us

profile of v3, /device:TPU:16, one launch (start us, length us, event | category | flops | bytes accessed | tf_op | source)
XLA Modules:
  0.0 32.2 jit_solution(6332045887235018563)
XLA Ops:
  0.0 31.5 %shard_map.55 = bf16[32,3072]{1,0:T(8,128)(2,1)S(1)} custom-call(s32[16]{0:T(128)} %counts_ref.1, bf16[64,768]{1,0:T(8,128)(2,1)} %q_ref.1, bf16[64,768]{1,0:T(8,128)(2,1)} %k_hbm.1, bf16[64,768]{1,0:T(8,128)(2,1)} %v_hbm.1, bf16[768,3072]{1,0:T(8,128)(2,1)} %wo_hbm.1), custom_call_target="tpu_custom_call" | custom-call | tf_op jit(solution)/shard_map/pallas_call | solution.py:423
  31.6 0.7 %copy.7 = bf16[32,3072]{1,0:T(8,128)(2,1)} copy(bf16[32,3072]{1,0:T(8,128)(2,1)S(1)} %shard_map.55) | data formatting | bytes 393216

commit v4 on v3

--- a/solution.py
+++ b/solution.py
@@ -12,7 +12,8 @@
 LAYER = 4
 NEG = -1e30
 MESH = pl.DeviceIdType.MESH
-UP, SIDE, CORE, CROSS = 0, 1, 2, 3
+KEYS, VALUES = 0, 1
+UP, SIDE, CORE, CROSS, UP_SIDE = 0, 1, 2, 3, 4
 
 
 def group_levels(levels):
@@ -171,30 +172,40 @@
             device_id_type=MESH,
         )
 
-    def forward_chain(step):
-        src = me - LAYER * step
-        for p in range(2):
-
-            @pl.when(step > 0)
-            def _():
-                piece(p, UP, step, src, above).wait_recv()
-
-            @pl.when(step == 0)
-            def _():
-                own[p].wait()
+    def send_own():
+        for p in (VALUES, KEYS):
+            own[p].wait()
 
             @pl.when(has_above)
             def _():
-                piece(p, UP, step, src, above).start()
-
+                piece(p, UP, 0, me, above).start()
+
+        for p in (KEYS, VALUES):
+            piece(p, SIDE, 0, me, side_dev).start()
+            piece(p, CORE, 0, me, core_dev).start()
+
+    def forward_chain(p, step):
+        src = me - LAYER * step
+        piece(p, UP, step, src, above).wait_recv()
+
+        @pl.when(has_above)
+        def _():
+            piece(p, UP, step, src, above).start()
+
+        if p == VALUES:
             piece(p, SIDE, step, src, side_dev).start()
-            piece(p, CORE, step, src, core_dev).start()
-
-    def forward_side(step):
+        piece(p, CORE, step, src, core_dev).start()
+
+    def forward_side(p, step):
         src = base + side_y - LAYER * step
-        for p in range(2):
-            piece(p, CROSS, step, src, core_dev).wait_recv()
-            piece(p, CROSS, step, src, core_dev).start()
+        piece(p, CROSS, step, src, core_dev).wait_recv()
+        if p == KEYS:
+
+            @pl.when(has_above)
+            def _():
+                piece(p, UP_SIDE, step, src, above).start()
+
+        piece(p, CROSS, step, src, core_dev).start()
 
     def wait_core(step):
         for p in range(2):
@@ -254,6 +265,10 @@
     def attend_own(step):
         attend(step, lambda cols: q_ref[:, cols], run_max, run_acc, slice(0, tok_rows), True)
 
+    def turn(block):
+        missing = jnp.zeros((HEAD_DIM - block.shape[0], HEAD_DIM), jnp.float32)
+        return jnp.transpose(jnp.concatenate([block, missing], axis=0))
+
     spot = lax.broadcasted_iota(jnp.int32, (tok_rows, HEAD_DIM), 1)
     pack = 2 if guests % 2 == 0 else 1
 
@@ -288,7 +303,7 @@
                             guest_acc[j, :, head_cols[h]] = guest_sum[h, at, :HEAD_DIM].astype(
                                 jnp.bfloat16
                             )
-                        guest_stats[j] = stats
+                        guest_stats[j] = turn(stats)[: guest_stats.shape[1]]
                         answer(j, 0).start()
                         answer(j, 1).start()
                 return carry
@@ -303,18 +318,26 @@
         guest_max[...] = jnp.full(guest_max.shape, NEG, jnp.float32)
         guest_sum[...] = jnp.zeros(guest_sum.shape, jnp.float32)
 
-    forward_chain(0)
-    forward_side(0)
+    send_own()
+    forward_side(KEYS, 0)
 
     def body(step, carry):
-        forward_chain(step)
+        forward_chain(VALUES, step)
+        forward_side(VALUES, step - 1)
+        forward_chain(KEYS, step)
         wait_core(step - 1)
         attend_own(step - 1)
-        forward_side(step)
-        attend_guests(step - 1, False)
+        forward_side(KEYS, step)
         return carry
 
     lax.fori_loop(1, local + 1, body, 0)
+    forward_side(VALUES, local)
+
+    def early_guests(step, carry):
+        attend_guests(step, False)
+        return carry
+
+    lax.fori_loop(0, local, early_guests, 0)
     wait_core(local)
     attend_guests(local, True)
     attend_own(local)
@@ -325,9 +348,10 @@
         def _():
             answer(0, 1).wait_recv()
             answer(0, 0).wait_recv()
+            stats = turn(far_stats[...])[:tok_rows]
             for h in range(head_count):
-                far_max = far_stats[:, h : h + 1]
-                far_total = far_stats[:, head_count + h : head_count + h + 1]
+                far_max = stats[:, h : h + 1]
+                far_total = stats[:, head_count + h : head_count + h + 1]
                 old_max = run_max[h][:, :1]
                 new_max = jnp.maximum(old_max, far_max)
                 fade = jnp.exp2((old_max - new_max) * scale)
@@ -371,17 +395,21 @@
         kept[c] = part[half:]
 
     def drain(step, carry):
-        for p in range(2):
+        for p in (KEYS, VALUES):
 
             @pl.when(has_above)
             def _():
-                piece(p, UP, step, me - LAYER * step, above).wait_send()
-
-            piece(p, SIDE, step, me - LAYER * step, side_dev).wait_send()
-            piece(p, CORE, step, me - LAYER * step, core_dev).wait_send()
-            piece(p, CROSS, step, me - LAYER * step, core_dev).wait_send()
+                piece(p, UP, step, me, above).wait_send()
+                if p == KEYS:
+                    piece(p, UP_SIDE, step, me, above).wait_send()
+
+            if p == VALUES:
+                piece(p, SIDE, step, me, side_dev).wait_send()
+            piece(p, CORE, step, me, core_dev).wait_send()
+            piece(p, CROSS, step, me, core_dev).wait_send()
         return carry
 
+    piece(KEYS, SIDE, 0, me, side_dev).wait_send()
     lax.fori_loop(0, local + 1, drain, 0)
     if guests:
 
@@ -418,6 +446,7 @@
     levels = n // LAYER
     guests = levels - group_levels(levels)
     room = max(guests, 1)
+    stat_rows = -(-2 * head_count // 8) * 8
     vmem = pltpu.VMEM
     dma = pltpu.SemaphoreType.DMA
     return pl.pallas_call(
@@ -441,14 +470,14 @@
             vmem((head_count, room * tok_rows, HEAD_DIM), jnp.float32),
             vmem((head_count, room * tok_rows, 2 * HEAD_DIM), jnp.float32),
             vmem((room, tok_rows, columns), jnp.bfloat16),
-            vmem((room, tok_rows, HEAD_DIM), jnp.float32),
+            vmem((room, stat_rows, HEAD_DIM), jnp.float32),
             vmem((tok_rows, columns), jnp.bfloat16),
-            vmem((tok_rows, HEAD_DIM), jnp.float32),
+            vmem((stat_rows, HEAD_DIM), jnp.float32),
             vmem((tok_rows, columns), jnp.bfloat16),
             vmem((chunks, half, chunk), jnp.float32),
             vmem((chunks, half, chunk), jnp.bfloat16),
             vmem((chunks, half, chunk), jnp.bfloat16),
-            dma((4, 2, levels)),
+            dma((5, 2, levels)),
             dma((2, n)),
             dma((2,)),
             dma,

time: 32.4 us -> 29.1 us (0.90)
  Pallas kernels: 31.5 us -> 28 us
    pallas_call x1, Pallas kernels: 31.5 us -> 28 us  [on_device(): pl.pallas_call(functools.partial(kernel, n, chunk), out_shape=jax.ShapeDt...]
where the time goes in v4:
time: 29.1 us; the launch traced here: 28.6 us
  Pallas kernels  28 us (96%)
  local copies, waits for them, and re-layouts  0.68 us (2%)
    pallas_call x1, Pallas kernels, on_device(): pl.pallas_call(functools.partial(kernel, n, chunk), out_shape=jax.ShapeDt...  28 us
    unnamed x1, local copies, waits for them, and re-layouts  0.68 us

profile of v4, /device:TPU:16, one launch (start us, length us, event | category | flops | bytes accessed | tf_op | source)
XLA Modules:
  0.0 28.6 jit_solution(8184746273981636597)
XLA Ops:
  0.0 28.0 %shard_map.55 = bf16[32,3072]{1,0:T(8,128)(2,1)S(1)} custom-call(s32[16]{0:T(128)} %counts_ref.1, bf16[64,768]{1,0:T(8,128)(2,1)} %q_ref.1, bf16[64,768]{1,0:T(8,128)(2,1)} %k_hbm.1, bf16[64,768]{1,0:T(8,128)(2,1)} %v_hbm.1, bf16[768,3072]{1,0:T(8,128)(2,1)} %wo_hbm.1), custom_call_target="tpu_custom_call" | custom-call | tf_op jit(solution)/shard_map/pallas_call | solution.py:452
  28.0 0.7 %copy.7 = bf16[32,3072]{1,0:T(8,128)(2,1)} copy(bf16[32,3072]{1,0:T(8,128)(2,1)S(1)} %shard_map.55) | data formatting | bytes 393216

commit v5 on v3

v5 whole, which is shorter than its diff:
```python
import functools
import math

import jax
import jax.numpy as jnp
from jax import lax
from jax.experimental import pallas as pl
from jax.experimental.pallas import tpu as pltpu
from jax.sharding import PartitionSpec as P

HEAD_DIM = 128
LAYER = 4
NEG = -1e30
MESH = pl.DeviceIdType.MESH
KEYS, VALUES = 0, 1
UP, SIDE, CORE, CROSS, UP_SIDE = 0, 1, 2, 3, 4


def group_levels(levels):
    return levels // 2 if levels % 2 == 0 else levels


def wings_of(head_count):
    return 2 if head_count % 2 == 0 else 1


def kernel(
    n,
    chunk,
    counts_ref,
    q_hbm,
    k_hbm,
    v_hbm,
    wo_hbm,
    out_ref,
    q_ref,
    q_sem,
    k_all,
    v_all,
    wo_all,
    run_max,
    run_acc,
    guest_q,
    guest_max,
    guest_sum,
    guest_acc,
    guest_stats,
    far_acc,
    far_stats,
    attended,
    kept,
    outgoing,
    incoming,
    send_sem,
    recv_sem,
    local_sem,
    wo_sem,
    x_send_sem,
    x_recv_sem,
    q_send_sem,
    q_recv_sem,
    back_send_sem,
    back_recv_sem,
):
    tok_rows, columns = q_hbm.shape
    wings = wings_of(columns // HEAD_DIM)
    breadth = columns // wings
    last_wing = wings - 1
    head_count = columns // HEAD_DIM
    width = wo_hbm.shape[1]
    half = tok_rows // 2
    me = lax.axis_index("ctx")
    tp = lax.axis_index("tp")
    levels = n // LAYER
    group = group_levels(levels)
    guests = levels - group
    level = me // LAYER
    is_upper = level >= group
    local = lax.rem(level, group)
    is_host = level == (group - 1 if guests else levels)
    lane = lax.rem(me, LAYER)
    base = level * LAYER
    side_y = lax.rem(lane + 2, LAYER)
    core_lane = lane + 1 - 2 * lax.rem(lane, 2)
    cross_lane = lax.rem(core_lane + 2, LAYER)
    above = lax.rem(me + LAYER, n)
    below = lax.rem(me + n - LAYER, n)
    has_above = local < group - 1
    has_below = local > 0
    host = (group - 1) * LAYER + lane
    guest_slot = lax.rem(level, group)
    side_dev, core_dev = base + side_y, base + core_lane
    halls = (k_all, v_all)
    inputs = (k_hbm, v_hbm)

    wo_copy = pltpu.make_async_copy(wo_hbm, wo_all, wo_sem)
    wo_copy.start()

    def rows_of(src):
        return pl.ds(pl.multiple_of(src * tok_rows, tok_rows), tok_rows)

    q_copy = pltpu.make_async_copy(q_hbm, q_ref, q_sem)
    q_copy.start()

    def wing_cols(w):
        return slice(w * breadth, (w + 1) * breadth)

    own = [
        pltpu.make_async_copy(inputs[p], halls[p].at[rows_of(me)], local_sem.at[p])
        for p in range(2)
    ]
    for p in range(2):
        own[p].start()

    barrier = pltpu.get_barrier_semaphore()

    def greet(dev, other_tp):
        pl.semaphore_signal(barrier, inc=1, device_id=(dev, other_tp), device_id_type=MESH)

    @pl.when(has_above)
    def _():
        greet(above, tp)

    @pl.when(has_below)
    def _():
        greet(below, tp)

    greet(side_dev, tp)
    greet(core_dev, tp)
    greet(me, 1 - tp)

    @pl.when(is_upper)
    def _():
        greet(host, tp)

    @pl.when(is_host)
    def _():
        def greet_guest(j, carry):
            greet(me + LAYER * (1 + j), tp)
            return carry

        lax.fori_loop(0, guests, greet_guest, 0)

    pl.semaphore_wait(
        barrier,
        3
        + has_above.astype(jnp.int32)
        + has_below.astype(jnp.int32)
        + is_upper.astype(jnp.int32)
        + guests * is_host.astype(jnp.int32),
    )

    def ask(j, w):
        return pltpu.make_async_remote_copy(
            src_ref=q_ref.at[:, wing_cols(w)],
            dst_ref=guest_q.at[rows_of(j), wing_cols(w)],
            send_sem=q_send_sem.at[w],
            recv_sem=q_recv_sem.at[w, j],
            device_id=(host, tp),
            device_id_type=MESH,
        )

    def answer(j, p, w):
        source, target = (
            (guest_acc.at[j, :, wing_cols(w)], far_acc.at[:, wing_cols(w)]),
            (guest_stats.at[j, w], far_stats.at[w]),
        )[p]
        return pltpu.make_async_remote_copy(
            src_ref=source,
            dst_ref=target,
            send_sem=back_send_sem.at[p, w, j],
            recv_sem=back_recv_sem.at[p, w],
            device_id=(lax.rem(me + LAYER * (1 + j), n), tp),
            device_id_type=MESH,
        )

    q_copy.wait()
    if guests:

        @pl.when(is_upper)
        def _():
            for w in range(wings):
                ask(guest_slot, w).start()

    def piece(p, w, kind, step, src, dev):
        where = halls[p].at[rows_of(src), wing_cols(w)]
        return pltpu.make_async_remote_copy(
            src_ref=where,
            dst_ref=where,
            send_sem=send_sem.at[kind, p * wings + w, step],
            recv_sem=recv_sem.at[p * wings + w, src],
            device_id=(dev, tp),
            device_id_type=MESH,
        )

    def rise_own(p, w):
        @pl.when(has_above)
        def _():
            piece(p, w, UP, 0, me, above).start()

    def forward_chain(p, w, step):
        src = me - LAYER * step
        piece(p, w, UP, step, src, above).wait_recv()

        @pl.when(has_above)
        def _():
            piece(p, w, UP, step, src, above).start()

        if p == VALUES:
            piece(p, w, SIDE, step, src, side_dev).start()
        piece(p, w, CORE, step, src, core_dev).start()

    def forward_side(p, w, step):
        src = base + side_y - LAYER * step
        piece(p, w, CROSS, step, src, core_dev).wait_recv()
        if p == KEYS:

            @pl.when(has_above)
            def _():
                piece(p, w, UP_SIDE, step, src, above).start()

        piece(p, w, CROSS, step, src, core_dev).start()

    def wait_core(w, step):
        for p in range(2):
            for other in (core_lane, cross_lane):
                piece(p, w, CORE, step, base + other - LAYER * step, core_dev).wait_recv()

    span = LAYER * tok_rows
    col = lax.broadcasted_iota(jnp.int32, (1, span), 1)
    slot = col // tok_rows
    place = lax.rem(col, tok_rows)
    scale = math.log2(math.e) / math.sqrt(HEAD_DIM)
    ones = jnp.ones((span, HEAD_DIM), jnp.bfloat16)
    head_cols = [slice(h * HEAD_DIM, (h + 1) * HEAD_DIM) for h in range(head_count)]

    each = head_count // wings
    wing_heads = [range(w * each, (w + 1) * each) for w in range(wings)]

    def attend(step, query, max_ref, acc_ref, rows, causal, w):
        heads = wing_heads[w]
        cols_of = [head_cols[h] for h in heads]
        first = base - LAYER * step
        limit = jnp.zeros((1, span), jnp.int32)
        for f in range(LAYER):
            live = counts_ref[first + f]
            if causal:
                live = jnp.where(first + f <= me, live, 0)
            limit = jnp.where(slot == f, live, limit)
        allowed = place < limit
        keys_at = pl.ds(pl.multiple_of(first * tok_rows, span), span)
        scores = [
            lax.dot_general(
                query(cols),
                k_all[keys_at, cols],
                (((1,), (1,)), ((), ())),
                preferred_element_type=jnp.float32,
            )
            for cols in cols_of
        ]
        scores = [jnp.where(allowed, one, NEG) for one in scores]
        old_max = [max_ref[h, rows, :][:, :1] for h in heads]
        new_max = [
            jnp.maximum(old, jnp.max(one, axis=-1, keepdims=True))
            for old, one in zip(old_max, scores)
        ]
        weights = [
            jnp.exp2((one - top) * scale).astype(jnp.bfloat16)
            for one, top in zip(scores, new_max)
        ]
        added = [
            jnp.dot(
                one,
                jnp.concatenate([v_all[keys_at, cols], ones], axis=1),
                preferred_element_type=jnp.float32,
            )
            for one, cols in zip(weights, cols_of)
        ]
        for i, h in enumerate(heads):
            fade = jnp.exp2((old_max[i] - new_max[i]) * scale)
            max_ref[h, rows, :] = jnp.broadcast_to(new_max[i], (fade.shape[0], HEAD_DIM))
            acc_ref[h, rows, :] = fade * acc_ref[h, rows, :] + added[i]

    def attend_own(step, w):
        attend(step, lambda cols: q_ref[:, cols], run_max, run_acc, slice(0, tok_rows), True, w)

    def turn(block):
        missing = jnp.zeros((HEAD_DIM - block.shape[0], HEAD_DIM), jnp.float32)
        return jnp.transpose(jnp.concatenate([block, missing], axis=0))

    spot = lax.broadcasted_iota(jnp.int32, (tok_rows, HEAD_DIM), 1)
    pack = 2 if guests % 2 == 0 else 1

    def attend_guests(step, last, w):
        if not guests:
            return

        @pl.when(is_host)
        def _():
            def one(i, carry):
                block = guests // pack - 1 - i

                @pl.when(step == 0)
                def _():
                    for g in range(pack):
                        ask(block * pack + g, w).wait_recv()

                rows = pl.ds(pl.multiple_of(block * pack * tok_rows, tok_rows), pack * tok_rows)
                attend(
                    step, lambda cols: guest_q[rows, cols], guest_max, guest_sum, rows, False, w
                )
                if last:
                    for g in reversed(range(pack)):
                        j = block * pack + g
                        at = rows_of(j)
                        stats = jnp.zeros((tok_rows, HEAD_DIM), jnp.float32)
                        for i, h in enumerate(wing_heads[w]):
                            stats = jnp.where(spot == i, guest_max[h, at, :], stats)
                            stats = jnp.where(
                                spot == each + i, guest_sum[h, at, HEAD_DIM:], stats
                            )
                            guest_acc[j, :, head_cols[h]] = guest_sum[h, at, :HEAD_DIM].astype(
                                jnp.bfloat16
                            )
                        guest_stats[j, w] = turn(stats)[: guest_stats.shape[2]]
                        answer(j, 0, w).start()
                        answer(j, 1, w).start()
                return carry

            lax.fori_loop(0, guests // pack, one, 0)

    run_max[...] = jnp.full(run_max.shape, NEG, jnp.float32)
    run_acc[...] = jnp.zeros(run_acc.shape, jnp.float32)

    @pl.when(is_host)
    def _():
        guest_max[...] = jnp.full(guest_max.shape, NEG, jnp.float32)
        guest_sum[...] = jnp.zeros(guest_sum.shape, jnp.float32)

    for p in (VALUES, KEYS):
        own[p].wait()
    rise_own(VALUES, 0)
    rise_own(KEYS, 0)
    for p in (KEYS, VALUES):
        piece(p, 0, SIDE, 0, me, side_dev).start()
        piece(p, 0, CORE, 0, me, core_dev).start()
    if last_wing:
        rise_own(VALUES, 1)
        piece(KEYS, 1, SIDE, 0, me, side_dev).start()
        for p in (KEYS, VALUES):
            piece(p, 1, CORE, 0, me, core_dev).start()
    forward_side(KEYS, 0, 0)
    if last_wing:
        rise_own(KEYS, 1)

    @pl.when(has_below)
    def _():
        forward_chain(VALUES, 0, 1)

    if last_wing:
        piece(VALUES, 1, SIDE, 0, me, side_dev).start()

    def body(step, carry):
        forward_side(VALUES, 0, step - 1)
        forward_chain(KEYS, 0, step)
        if last_wing:
            forward_side(KEYS, 1, step - 1)
            forward_chain(VALUES, 1, step)
        forward_side(KEYS, 0, step)
        if last_wing:
            forward_chain(KEYS, 1, step)
            forward_side(VALUES, 1, step - 1)

        @pl.when(step < local)
        def _():
            forward_chain(VALUES, 0, step + 1)

        return carry

    lax.fori_loop(1, local + 1, body, 0)

    for w in range(wings):
        forward_side(VALUES, w, local)
        if w:
            forward_side(KEYS, w, local)

        def early(step, carry):
            wait_core(w, step)
            attend_guests(step, False, w)
            return carry

        lax.fori_loop(0, local, early, 0)
        wait_core(w, local)
        attend_guests(local, True, w)

    for w in range(wings):

        def own_step(step, carry):
            attend_own(step, w)
            return carry

        lax.fori_loop(0, local + 1, own_step, 0)

    if guests:

        @pl.when(is_upper)
        def _():
            for w in range(wings):
                answer(0, 0, w).wait_recv()
                answer(0, 1, w).wait_recv()
                stats = turn(far_stats[w])[:tok_rows]
                for i, h in enumerate(wing_heads[w]):
                    far_max = stats[:, i : i + 1]
                    far_total = stats[:, each + i : each + i + 1]
                    old_max = run_max[h][:, :1]
                    new_max = jnp.maximum(old_max, far_max)
                    fade = jnp.exp2((old_max - new_max) * scale)
                    far_fade = jnp.exp2((far_max - new_max) * scale)
                    far = jnp.concatenate(
                        [
                            far_acc[:, head_cols[h]].astype(jnp.float32),
                            jnp.broadcast_to(far_total, (tok_rows, HEAD_DIM)),
                        ],
                        axis=1,
                    )
                    run_acc[h] = fade * run_acc[h] + far_fade * far

    row = lax.broadcasted_iota(jnp.int32, (tok_rows, HEAD_DIM), 0)
    row_live = row < counts_ref[me]
    for h in range(head_count):
        out = jnp.where(row_live, run_acc[h, :, :HEAD_DIM] / run_acc[h, :, HEAD_DIM:], 0.0)
        attended[:, head_cols[h]] = out.astype(jnp.bfloat16)

    wo_copy.wait()
    theirs = attended[pl.ds(pl.multiple_of((1 - tp) * half, half), half), :]
    mine = attended[pl.ds(pl.multiple_of(tp * half, half), half), :]
    lhs = jnp.concatenate([theirs, mine], axis=0)

    def swap(c):
        return pltpu.make_async_remote_copy(
            src_ref=outgoing.at[c],
            dst_ref=incoming.at[c],
            send_sem=x_send_sem.at[c],
            recv_sem=x_recv_sem.at[c],
            device_id=(me, 1 - tp),
            device_id_type=MESH,
        )

    for c in range(width // chunk):
        part = jnp.dot(
            lhs, wo_all[:, c * chunk : (c + 1) * chunk], preferred_element_type=jnp.float32
        )
        outgoing[c] = part[:half].astype(jnp.bfloat16)
        swap(c).start()
        kept[c] = part[half:]

    def drain(step, carry):
        for w in range(wings):
            for p in (KEYS, VALUES):

                @pl.when(has_above)
                def _():
                    piece(p, w, UP, step, me, above).wait_send()
                    if p == KEYS:
                        piece(p, w, UP_SIDE, step, me, above).wait_send()

                if p == VALUES:
                    piece(p, w, SIDE, step, me, side_dev).wait_send()
                piece(p, w, CORE, step, me, core_dev).wait_send()
                piece(p, w, CROSS, step, me, core_dev).wait_send()
        return carry

    for w in range(wings):
        piece(KEYS, w, SIDE, 0, me, side_dev).wait_send()
    lax.fori_loop(0, local + 1, drain, 0)
    if guests:

        @pl.when(is_upper)
        def _():
            for w in range(wings):
                ask(guest_slot, w).wait_send()

        @pl.when(is_host)
        def _():
            def drain_guest(j, carry):
                for w in range(wings):
                    answer(j, 0, w).wait_send()
                    answer(j, 1, w).wait_send()
                return carry

            lax.fori_loop(0, guests, drain_guest, 0)

    for c in range(width // chunk):
        swap(c).wait_recv()
        out_ref[:, c * chunk : (c + 1) * chunk] = (
            kept[c] + incoming[c].astype(jnp.float32)
        ).astype(out_ref.dtype)
    for c in range(width // chunk):
        swap(c).wait_send()


def on_device(queries, keys, values, wo, frame_tokens):
    tok_rows, columns = queries.shape
    width = wo.shape[1]
    n = lax.axis_size("ctx")
    half = tok_rows // 2
    chunk = 256 if width % 256 == 0 else width
    chunks = width // chunk
    head_count = columns // HEAD_DIM
    levels = n // LAYER
    guests = levels - group_levels(levels)
    room = max(guests, 1)
    wings = wings_of(head_count)
    stat_rows = -(-2 * head_count // wings // 8) * 8
    vmem = pltpu.VMEM
    dma = pltpu.SemaphoreType.DMA
    return pl.pallas_call(
        functools.partial(kernel, n, chunk),
        out_shape=jax.ShapeDtypeStruct((half, width), jnp.bfloat16),
        in_specs=[
            pl.BlockSpec(memory_space=pltpu.SMEM),
            pl.BlockSpec(memory_space=pltpu.HBM),
            pl.BlockSpec(memory_space=pltpu.HBM),
            pl.BlockSpec(memory_space=pltpu.HBM),
            pl.BlockSpec(memory_space=pltpu.HBM),
        ],
        out_specs=pl.BlockSpec(memory_space=vmem),
        scratch_shapes=[
            vmem((tok_rows, columns), jnp.bfloat16),
            dma,
            vmem((n * tok_rows, columns), jnp.bfloat16),
            vmem((n * tok_rows, columns), jnp.bfloat16),
            vmem(wo.shape, jnp.bfloat16),
            vmem((head_count, tok_rows, HEAD_DIM), jnp.float32),
            vmem((head_count, tok_rows, 2 * HEAD_DIM), jnp.float32),
            vmem((room * tok_rows, columns), jnp.bfloat16),
            vmem((head_count, room * tok_rows, HEAD_DIM), jnp.float32),
            vmem((head_count, room * tok_rows, 2 * HEAD_DIM), jnp.float32),
            vmem((room, tok_rows, columns), jnp.bfloat16),
            vmem((room, wings, stat_rows, HEAD_DIM), jnp.float32),
            vmem((tok_rows, columns), jnp.bfloat16),
            vmem((wings, stat_rows, HEAD_DIM), jnp.float32),
            vmem((tok_rows, columns), jnp.bfloat16),
            vmem((chunks, half, chunk), jnp.float32),
            vmem((chunks, half, chunk), jnp.bfloat16),
            vmem((chunks, half, chunk), jnp.bfloat16),
            dma((5, 2 * wings, levels)),
            dma((2 * wings, n)),
            dma((2,)),
            dma,
            dma((chunks,)),
            dma((chunks,)),
            dma((wings,)),
            dma((wings, room)),
            dma((2, wings, room)),
            dma((2, wings)),
        ],
        compiler_params=pltpu.CompilerParams(
            collective_id=0, has_side_effects=True, vmem_limit_bytes=52 << 20
        ),
    )(*[pltpu.with_memory_space_constraint(x, pltpu.HBM) for x in (frame_tokens, queries, keys, values, wo)])


def solution(mesh):
    in_specs = (P("ctx", "tp"), P("ctx", "tp"), P("ctx", "tp"), P("tp", None), P())
    out_specs = P(("ctx", "tp"), None)
    return jax.shard_map(
        on_device, mesh=mesh, in_specs=in_specs, out_specs=out_specs, check_vma=False
    )
```

time: 32.4 us -> 28.9 us (0.89)
  Pallas kernels: 31.5 us -> 28 us
    pallas_call x1, Pallas kernels: 31.5 us -> 28 us  [on_device(): pl.pallas_call(functools.partial(kernel, n, chunk), out_shape=jax.ShapeDt...]
where the time goes in v5:
time: 28.9 us; the launch traced here: 28.7 us
  Pallas kernels  28 us (97%)
  local copies, waits for them, and re-layouts  0.68 us (2%)
    pallas_call x1, Pallas kernels, on_device(): pl.pallas_call(functools.partial(kernel, n, chunk), out_shape=jax.ShapeDt...  28 us
    unnamed x1, local copies, waits for them, and re-layouts  0.68 us

profile of v5, /device:TPU:16, one launch (start us, length us, event | category | flops | bytes accessed | tf_op | source)
XLA Modules:
  0.0 28.7 jit_solution(12631748107970756007)
XLA Ops:
  0.0 28.0 %shard_map.55 = bf16[32,3072]{1,0:T(8,128)(2,1)S(1)} custom-call(s32[16]{0:T(128)} %counts_ref.1, bf16[64,768]{1,0:T(8,128)(2,1)} %q_hbm.1, bf16[64,768]{1,0:T(8,128)(2,1)} %k_hbm.1, bf16[64,768]{1,0:T(8,128)(2,1)} %v_hbm.1, bf16[768,3072]{1,0:T(8,128)(2,1)} %wo_hbm.1), custom_call_target="tpu_custom_call" | custom-call | tf_op jit(solution)/shard_map/pallas_call | solution.py:517
  28.0 0.7 %copy.7 = bf16[32,3072]{1,0:T(8,128)(2,1)} copy(bf16[32,3072]{1,0:T(8,128)(2,1)S(1)} %shard_map.55) | data formatting | bytes 393216

commit v6 on v5

--- a/solution.py
+++ b/solution.py
@@ -504,7 +504,7 @@
     width = wo.shape[1]
     n = lax.axis_size("ctx")
     half = tok_rows // 2
-    chunk = 256 if width % 256 == 0 else width
+    chunk = 512 if width % 512 == 0 else width
     chunks = width // chunk
     head_count = columns // HEAD_DIM
     levels = n // LAYER

time: 28.9 us -> 28.6 us (0.990)
  no operation moved by 1% of the time
where the time goes in v6:
time: 28.6 us; the launch traced here: 28.5 us
  Pallas kernels  27.8 us (97%)
  local copies, waits for them, and re-layouts  0.68 us (2%)
    pallas_call x1, Pallas kernels, on_device(): pl.pallas_call(functools.partial(kernel, n, chunk), out_shape=jax.ShapeDt...  27.8 us
    unnamed x1, local copies, waits for them, and re-layouts  0.68 us

profile of v6, /device:TPU:16, one launch (start us, length us, event | category | flops | bytes accessed | tf_op | source)
XLA Modules:
  0.0 28.5 jit_solution(15081514477486144690)
XLA Ops:
  0.0 27.8 %shard_map.55 = bf16[32,3072]{1,0:T(8,128)(2,1)S(1)} custom-call(s32[16]{0:T(128)} %counts_ref.1, bf16[64,768]{1,0:T(8,128)(2,1)} %q_hbm.1, bf16[64,768]{1,0:T(8,128)(2,1)} %k_hbm.1, bf16[64,768]{1,0:T(8,128)(2,1)} %v_hbm.1, bf16[768,3072]{1,0:T(8,128)(2,1)} %wo_hbm.1), custom_call_target="tpu_custom_call" | custom-call | tf_op jit(solution)/shard_map/pallas_call | solution.py:517
  27.8 0.7 %copy.7 = bf16[32,3072]{1,0:T(8,128)(2,1)} copy(bf16[32,3072]{1,0:T(8,128)(2,1)S(1)} %shard_map.55) | data formatting | bytes 393216
